TPU v7x, 256 devices: a whole 4x4x8 slice. The times are simulated.
256 devices in a mesh: tm: 4 (over x_hi, core), space: 64 (over z, x_lo, y).
Axes of the slice: x: 4 (x_hi: 2, x_lo: 2; x = x_hi * 2 + x_lo), y: 4, z: 8, core: 2. Of those that a mesh axis runs over, the one named last changes fastest.
Arguments:
- queries: bfloat16 [4, 4, 64, 32, 1536], P('tm', None, 'space'), may hold values from -30 to 30
- key_states: bfloat16 [4, 4, 64, 32, 1536], P('tm', None, 'space'), may hold values from -30 to 30, as said below
- value_states: bfloat16 [4, 4, 64, 32, 1536], P('tm', None, 'space'), may hold values from -6 to 6
- conv_weight: float32 [3, 3, 3, 1536], replicated, may hold values from -0.3125 to 0.3125
Outputs:
- mixed: bfloat16 [4, 4, 64, 32, 1536], P('tm', None, 'space')
Inputs may be any that keep to these rules, and one draw needn't show every extreme that they name: `key_states`: entries are real-valued keys.
All inputs are finite; a program needn't handle non-finite values.
Results may differ from a plain program's by a relative error of at most 0.0088.
Values may be sent and summed in bfloat16 or wider, within the bound.
No kernel may reach another device: no remote copies, remote signals or barrier semaphores. Data moves between devices by JAX's collectives and lax.ppermute only.
A program may use at most 192 MiB of HBM per device.

v0:
```python
import math
import jax
import jax.numpy as jnp
from jax import lax
from jax.sharding import PartitionSpec as P

HEADS = 24
HEAD_DIM = 64
D = 1536
FRAMES = 4
ROWS_DEV = 1
COLUMNS = 32
AGENT_DEV = 4


def extended(cells, sides, width):
    for axis, dim in sides:
        count = lax.axis_size(axis)
        ends = count - 1
        head = lax.slice_in_dim(cells, 0, width, axis=dim)
        tail = lax.slice_in_dim(cells, cells.shape[dim] - width, cells.shape[dim], axis=dim)
        cells = jnp.concatenate(
            [
                lax.ppermute(tail, axis, [(i, (i + 1) % count) for i in range(ends)]),
                cells,
                lax.ppermute(head, axis, [((i + 1) % count, i) for i in range(ends)]),
            ],
            axis=dim,
        )
    return cells


def mix_local(window, conv_weight):
    shape = (window.shape[0] - 2, window.shape[1] - 2, window.shape[2] - 2, window.shape[3])
    total = jnp.zeros(shape, jnp.float32)
    for time_off in range(3):
        for row_off in range(3):
            for col_off in range(3):
                piece = window[
                    time_off : time_off + shape[0],
                    row_off : row_off + shape[1],
                    col_off : col_off + shape[2],
                ]
                total = total + piece.astype(jnp.float32) * conv_weight[time_off, row_off, col_off]
    return total


def on_device(queries, key_states, value_states, conv_weight):
    tokens = FRAMES * ROWS_DEV * COLUMNS
    inv_root = HEAD_DIM ** (-0.5)
    per_block = math.gcd(HEADS, 8)
    blocks = HEADS // per_block
    padded = extended(value_states, (("tm", 1), ("space", 2)), 1)
    window = jnp.pad(padded[0], ((0, 0), (0, 0), (1, 1), (0, 0)))
    pooled = jnp.mean(
        queries.reshape(FRAMES, ROWS_DEV, AGENT_DEV, COLUMNS // AGENT_DEV, D),
        axis=(0, 1, 3),
        dtype=jnp.float32,
    )
    agents = lax.all_gather(pooled.astype(jnp.bfloat16), "space", axis=0, tiled=True)
    count = agents.shape[0]
    agent_heads = agents.reshape(count, HEADS, HEAD_DIM)
    query_heads = queries.reshape(tokens, HEADS, HEAD_DIM)
    key_heads = key_states.reshape(tokens, HEADS, HEAD_DIM)
    value_heads = value_states.reshape(tokens, HEADS, HEAD_DIM)

    def agent_block(index):
        start = index * per_block
        agent_part = lax.dynamic_slice_in_dim(agent_heads, start, per_block, 1)
        key_part = lax.dynamic_slice_in_dim(key_heads, start, per_block, 1)
        value_part = lax.dynamic_slice_in_dim(value_heads, start, per_block, 1)
        scores = (
            jnp.einsum("ahd,nhd->ahn", agent_part, key_part, preferred_element_type=jnp.float32)
            * inv_root
        )
        block_peak = jnp.max(scores, axis=2)
        weights = jnp.exp(scores - block_peak[..., None])
        block_total = jnp.sum(weights, axis=2)
        block_acc = jnp.einsum(
            "ahn,nhd->ahd",
            weights.astype(jnp.bfloat16),
            value_part,
            preferred_element_type=jnp.float32,
        )
        return (block_peak, block_total, block_acc)

    peaks, totals, accs = lax.map(agent_block, jnp.arange(blocks, dtype=jnp.int32))
    local_peak = peaks.transpose(1, 0, 2).reshape(count, HEADS)
    local_total = totals.transpose(1, 0, 2).reshape(count, HEADS)
    local_acc = accs.transpose(1, 0, 2, 3).reshape(count, HEADS, HEAD_DIM)
    peak = lax.pmax(local_peak, "space")
    rescale = jnp.exp(local_peak - peak)
    total_sum, acc_sum = lax.psum((local_total * rescale, local_acc * rescale[..., None]), "space")
    agent_values = (acc_sum / total_sum[..., None]).astype(jnp.bfloat16)

    def query_block(index):
        start = index * per_block
        query_part = lax.dynamic_slice_in_dim(query_heads, start, per_block, 1)
        agent_part = lax.dynamic_slice_in_dim(agent_heads, start, per_block, 1)
        values_part = lax.dynamic_slice_in_dim(agent_values, start, per_block, 1)
        query_scores = (
            jnp.einsum("nhd,ahd->hna", query_part, agent_part, preferred_element_type=jnp.float32)
            * inv_root
        )
        probs = jax.nn.softmax(query_scores, axis=-1).astype(jnp.bfloat16)
        return jnp.einsum("hna,ahd->nhd", probs, values_part, preferred_element_type=jnp.float32)

    outputs = lax.map(query_block, jnp.arange(blocks, dtype=jnp.int32))
    attended = outputs.transpose(1, 0, 2, 3).reshape(FRAMES, ROWS_DEV, COLUMNS, D)
    local_mix = mix_local(window, conv_weight)
    mixed = (attended + local_mix).astype(jnp.bfloat16)
    return mixed.reshape(value_states.shape)


def solution(mesh):
    return jax.shard_map(
        on_device,
        mesh=mesh,
        in_specs=(
            P("tm", None, "space", None, None),
            P("tm", None, "space", None, None),
            P("tm", None, "space", None, None),
            P(),
        ),
        out_specs=P("tm", None, "space", None, None),
        check_vma=False,
    )
```

profile of v0, /device:TPU:4, one launch (start us, length us, event | category | flops | bytes accessed | tf_op | source)
XLA Modules:
  0.0 1130.5 jit_solution(9148870399939223260)
XLA Ops:
  6.5 1.6 reshape.95
  8.2 0.5 copy.36
  8.8 162.9 %all-gather = bf16[64,4,1536]{2,1,0:T(4,128)(2,1)S(1)} all-gather(bf16[1,4,1536]{2,1,0:T(4,128)(2,1)S(1)} %fusion.47), channel_id=1, replica_groups=mesh['tm'=4,'space'=64] {'space'}, dimensions={0}, use_global_device_ids=true | all-gather | bytes 798720 | tf_op jit(solution)/shard_map/all_gather | solution.py:60
  171.7 0.8 reshape.96
  172.6 1.0 copy.37
  173.6 0.4 reshape.97
  174.0 0.5 copy.38
  174.5 9.1 while.24
  174.5 0.7 dynamic_slice.74
  175.9 0.4 fusion.69
  176.5 1.1 fusion.71
  177.6 0.7 dynamic_slice.74
  178.9 0.4 fusion.69
  179.5 1.1 fusion.71
  180.6 0.7 dynamic_slice.74
  182.0 0.4 fusion.69
  182.3 0.2 fusion.70
  182.5 1.1 fusion.71
  183.6 302.7 %pmax.7 = f32[256,24]{0,1:T(8,128)S(1)} all-reduce(f32[256,24]{0,1:T(8,128)S(1)} %bitcast.68), channel_id=1, replica_groups=mesh['tm'=4,'space'=64] {'space'}, use_global_device_ids=true, to_apply=%region_6.7 | all-reduce | flops 6144 | bytes 49152 | tf_op jit(solution)/shard_map/pmax | solution.py:91
  486.4 0.6 bitcast_multiply_fusion.1
  487.0 2.8 bitcast_multiply_fusion
  489.8 2.1 collective-permute-start.1
  491.8 2.4 collective-permute-start
  494.2 5.5 collective-permute-done.1
  499.8 1.9 collective-permute-done
  501.7 1.3 collective-permute-start.3
  503.0 5.4 collective-permute-start.2
  508.4 0.4 reshape.101
  508.9 1.2 copy.39
  510.1 302.9 %psum.15 = f32[256,24]{0,1:T(8,128)} all-reduce(f32[256,24]{0,1:T(8,128)} %get-tuple-element.182), channel_id=1, replica_groups=mesh['tm'=4,'space'=64] {'space'}, use_global_device_ids=true, to_apply=%region_8.9 | all-reduce | flops 6144 | bytes 49152 | tf_op jit(solution)/shard_map/psum | solution.py:93
  813.0 1.6 slice_reduce_fusion.25
  814.6 2.0 slice_reduce_fusion.26
  816.6 1.4 maximum_bitcast_fusion
  818.0 279.5 %all-reduce.3.cloned.1.call-done = f32[256,24,64]{0,2,1:T(8,128)} async-done(((f32[256,24,64]{0,2,1:T(8,128)}), f32[256,24,64]{0,2,1:T(8,128)}) %all-reduce.3.cloned.1.call-update) | async-done | bytes 1572880 | tf_op jit(solution)/shard_map/psum | solution.py:93
  1097.5 1.6 divide_convert_fusion.2
  1099.1 15.7 %while.25 = (s32[]{:T(128)}, f32[3,128,8,64]{1,3,2,0:T(8,128)}, s32[3]{0:T(128)S(1)}, bf16[256,24,64]{0,2,1:T(8,128)(2,1)S(1)}, bf16[128,24,64]{0,2,1:T(8,128)(2...) while((s32[]{:T(128)}, f32[3,128,8,64]{1,3,2,0:T(8,128)}, ...), condition=%wide.region_12.13_spmd, body=%wide.region_9.12_spmd.sunk | while | flops 102499840 | bytes 1322151 | solution.py:108
  1099.1 0.6 dynamic_slice.80
  1100.4 1.6 fusion.77
  1102.0 2.4 fusion.78
  1104.4 0.6 dynamic_slice.80
  1105.6 1.6 fusion.77
  1107.2 2.4 fusion.78
  1109.6 0.6 dynamic_slice.80
  1110.9 1.6 fusion.77
  1112.4 2.4 fusion.78
  1114.9 1.7 copy.41
  1116.8 1.3 reshape.102
  1118.3 5.4 fusion.46
  (78 shorter events, 0.7 us)
Async XLA Ops:
  6.5 2.1 copy-start.1
  6.5 1091.0 %all-reduce.3.cloned.1.call-start = ((), (), s32[]{:S(2)}) async-start(), calls=%async_computation | async-start | bytes 3145728 | tf_op jit(solution)/shard_map/psum | solution.py:93
  172.5 1.0 copy-start
  489.7 18.7 %copy-start.2 = (bf16[1,4,1,32,1536]{4,3,2,1,0:T(8,128)(2,1)S(1)}, bf16[1,4,1,32,1536]{4,3,2,1,0:T(8,128)(2,1)}, u32[]{:S(2)}) copy-start(bf16[1,4,1,32,1536]{4,3,2,1,0:T(8,128)(2,1)} %param.8) | copy-start | bytes 1179652
  489.8 10.0 collective-permute-start.1
  491.8 9.8 collective-permute-start
  499.8 1.9 copy-start.3
  501.6 1.4 copy-start.4
  501.7 314.9 %collective-permute-start.3 = (bf16[1,6,1,32,1536]{4,3,1,2,0:T(8,128)(2,1)S(1)}, bf16[1,6,1,32,1536]{4,3,1,2,0:T(8,128)(2,1)S(1)}, u32[]{:S(2)}, u32[]{:S(2)}) collective-permute-start(bf16[1,6,1,32,1536]{4,3,1,2,0:T(8,128)(2,1)S(1)} %pad_maximum_fusion), channel_id=1, source_target_pairs={{1,0},{2,1},{3,2},{4,3},{5,4},{6,5},{7,6},{8,7},{9,8},{10,9},{11,1... | collective-permute-start | bytes 1769480 | tf_op jit(solution)/shard_map/ppermute | solution.py:26
  503.0 313.6 %collective-permute-start.2 = (bf16[1,6,1,32,1536]{4,3,1,2,0:T(8,128)(2,1)S(1)}, bf16[1,6,1,32,1536]{4,3,1,2,0:T(8,128)(2,1)}, u32[]{:S(2)}, u32[]{:S(2)}) collective-permute-start(bf16[1,6,1,32,1536]{4,3,1,2,0:T(8,128)(2,1)S(1)} %pad_maximum_fusion), channel_id=1, source_target_pairs={{0,1},{1,2},{2,3},{3,4},{4,5},{5,6},{6,7},{7,8},{8,9},{9,10},{10,1... | collective-permute-start | bytes 1769480 | tf_op jit(solution)/shard_map/ppermute | solution.py:24
  1116.5 1.5 copy-start.5
  1116.5 1.5 copy-start.6
  1116.6 1.5 copy-start.7
  1116.6 1.5 copy-start.8
  1116.6 1.5 copy-start.9
  1116.6 1.5 copy-start.10
  1116.6 1.5 copy-start.11
  1116.6 1.5 copy-start.12
  1116.6 1.5 copy-start.13
  1116.6 1.5 copy-start.14
  1116.6 1.5 copy-start.15
  1116.6 1.5 copy-start.16
  1116.7 1.5 copy-start.17
  1116.7 1.5 copy-start.18
  1116.7 1.5 copy-start.19
  1116.7 1.5 copy-start.20
  1116.7 1.5 copy-start.21
  1116.7 1.5 copy-start.22
  1116.7 1.5 copy-start.23
  1116.7 1.5 copy-start.24
  1116.7 1.5 copy-start.25
  1116.7 1.5 copy-start.26
  1116.8 1.5 copy-start.27
  1116.8 1.5 copy-start.28
Sparse Core Ops, SparseCore 0:
  489.9 607.6 all-reduce.2
where the time goes:
time: 1130 us
  blocking collectives  769 us (68%)
  waiting for transfers between devices  287 us (25%)
  local copies, waits for them, and re-layouts  17.1 us (2%)
  matrix products  16.4 us (1%)
  between operations  13.9 us (1%)
  other arithmetic  12.4 us (1%)
    psum x1, blocking collectives, on_device(): lax.psum((local_total * rescale, local_acc * rescale[..., None]), 'space')  303 us
    pmax x1, blocking collectives, on_device(): peak = lax.pmax(local_peak, 'space')  303 us
    psum x1, waiting for transfers between devices, on_device(): lax.psum((local_total * rescale, local_acc * rescale[..., None]), 'space')  280 us
    all_gather x1, blocking collectives, on_device(): lax.all_gather(pooled.astype(jnp.bfloat16), 'space', axis=0, tiled=True)  163 us
  transfers between devices with their start and end apart: 5, of which 3 were waited for; matrix products, arithmetic and copies ran while one was open for 1% of the time, Pallas kernels for 0%

commit v1 on v0

--- a/solution.py
+++ b/solution.py
@@ -11,6 +11,13 @@
 ROWS_DEV = 1
 COLUMNS = 32
 AGENT_DEV = 4
+
+
+def gather_over(array, mesh_axis, d):
+    size = lax.axis_size(mesh_axis)
+    tiles = jnp.stack([array for _ in range(size)])
+    tiles = lax.all_to_all(tiles, mesh_axis, split_axis=0, concat_axis=0)
+    return jnp.concatenate(tiles, axis=d)
 
 
 def extended(cells, sides, width):
@@ -57,7 +64,7 @@
         axis=(0, 1, 3),
         dtype=jnp.float32,
     )
-    agents = lax.all_gather(pooled.astype(jnp.bfloat16), "space", axis=0, tiled=True)
+    agents = gather_over(pooled.astype(jnp.bfloat16), "space", 0)
     count = agents.shape[0]
     agent_heads = agents.reshape(count, HEADS, HEAD_DIM)
     query_heads = queries.reshape(tokens, HEADS, HEAD_DIM)

time: 1130 us -> 1010 us (0.89)
  blocking collectives: 769 us -> 611 us
  waiting for transfers between devices: 287 us -> 306 us
  starting transfers between devices: 11.1 us -> 23.9 us
    all_gather x1 -> x0, blocking collectives: 163 us -> none  [on_device(): lax.all_gather(pooled.astype(jnp.bfloat16), 'space', axis=0, tiled=True)]
    all_to_all x0 -> x1, waiting for transfers between devices: none -> 20.4 us  [gather_over(): tiles = lax.all_to_all(tiles, mesh_axis, split_axis=0, concat_axis=0)]
    all_to_all x0 -> x1, starting transfers between devices: none -> 12.7 us  [gather_over(): tiles = lax.all_to_all(tiles, mesh_axis, split_axis=0, concat_axis=0)]
  transfers between devices with their start and end apart: 5 -> 6, of which waited for: 3 -> 6; matrix products, arithmetic and copies ran while one was open for 1% -> 1% of each run, Pallas kernels for 0% -> 0%
where the time goes in v1:
time: 1010 us
  blocking collectives  611 us (60%)
  waiting for transfers between devices  306 us (30%)
  starting transfers between devices  23.9 us (2%)
  matrix products  19.1 us (2%)
  local copies, waits for them, and re-layouts  17.6 us (2%)
  between operations  14 us (1%)
  other arithmetic  13.5 us (1%)
    psum x1, blocking collectives, on_device(): lax.psum((local_total * rescale, local_acc * rescale[..., None]), 'space')  306 us
    pmax x1, blocking collectives, on_device(): peak = lax.pmax(local_peak, 'space')  305 us
    psum x1, waiting for transfers between devices, on_device(): lax.psum((local_total * rescale, local_acc * rescale[..., None]), 'space')  278 us
    all_to_all x1, waiting for transfers between devices, gather_over(): tiles = lax.all_to_all(tiles, mesh_axis, split_axis=0, concat_axis=0)  20.4 us
  transfers between devices with their start and end apart: 6, of which 6 were waited for; matrix products, arithmetic and copies ran while one was open for 1% of the time, Pallas kernels for 0%

profile of v1, /device:TPU:4, one launch (start us, length us, event | category | flops | bytes accessed | tf_op | source)
XLA Modules:
  0.0 1008.7 jit_solution(16076439362693872958)
XLA Ops:
  6.5 1.1 convert_reduce_fusion
  7.7 1.1 stack.2
  8.8 12.7 %all-to-all-start = ((bf16[64,4,1536]{2,1,0:T(4,128)(2,1)}), bf16[64,4,1536]{2,1,0:T(4,128)(2,1)S(1)}, u32[]{:S(2)}, u32[]{:S(2)}) async-start(bf16[64,4,1536]{2,1,0:T(4,128)(2,1)} %stack.2), calls=%async_computation | async-start | bytes 1572864 | tf_op jit(solution)/shard_map/all_to_all | solution.py:19
  21.7 0.4 reshape.94
  22.1 0.5 copy.25
  22.6 0.4 reshape.95
  23.1 1.2 copy.27
  24.3 20.4 %all-to-all-done = bf16[64,4,1536]{2,1,0:T(4,128)(2,1)S(1)} async-done(((bf16[64,4,1536]{2,1,0:T(4,128)(2,1)}), bf16[64,4,1536]{2,1,0:T(4,128)(2,1)S(1)}, u32[]{:S(2)}, u32[]{:S(2)}) %all-to-all-start) | async-done | bytes 786464 | tf_op jit(solution)/shard_map/all_to_all | solution.py:19
  44.7 0.8 reshape_reshape.3
  45.5 1.0 copy.26
  46.5 11.1 %while.24 = (s32[]{:T(128)}, f32[3,256,8]{1,2,0:T(8,128)S(1)}, f32[3,256,8]{1,2,0:T(8,128)S(1)}, f32[3,256,8,64]{1,3,2,0:T(8,128)}, s32[3]{0:T(128)S(1)}, /*inde...) while((s32[]{:T(128)}, f32[3,256,8]{1,2,0:T(8,128)S(1)}, ...), condition=%wide.region_5.6_spmd, body=%wide.region_2.5_spmd.sunk | while | flops 68677632 | bytes 4261059 | solution.py:94
  46.5 0.6 dynamic_slice.74
  48.2 2.0 fusion.70
  50.2 0.6 dynamic_slice.74
  51.8 2.0 fusion.70
  53.9 0.6 dynamic_slice.74
  55.5 2.0 fusion.70
  57.6 305.1 %pmax.7 = f32[256,24]{0,1:T(8,128)S(1)} all-reduce(f32[256,24]{0,1:T(8,128)S(1)} %bitcast.67), channel_id=1, replica_groups=mesh['tm'=4,'space'=64] {'space'}, use_global_device_ids=true, to_apply=%region_6.7 | all-reduce | flops 6144 | bytes 49152 | tf_op jit(solution)/shard_map/pmax | solution.py:98
  362.6 0.6 bitcast_multiply_fusion.1
  363.3 2.8 bitcast_multiply_fusion
  366.1 2.1 collective-permute-start.1
  368.1 2.4 collective-permute-start
  370.5 3.5 collective-permute-done.1
  374.0 1.6 collective-permute-done
  375.7 1.3 collective-permute-start.3
  377.0 5.4 collective-permute-start.2
  382.8 1.2 copy.28
  384.0 1.7 slice_reduce_fusion.25
  385.7 2.2 slice_reduce_fusion.26
  387.9 1.9 collective-permute-done.3
  389.8 1.1 collective-permute-done.2
  390.9 1.4 maximum_bitcast_fusion
  392.3 305.8 %psum.15 = f32[256,24]{0,1:T(8,128)S(1)} all-reduce(f32[256,24]{0,1:T(8,128)} %get-tuple-element.168), channel_id=1, replica_groups=mesh['tm'=4,'space'=64] {'space'}, use_global_device_ids=true, to_apply=%region_8.9 | all-reduce | flops 6144 | bytes 49152 | tf_op jit(solution)/shard_map/psum | solution.py:100
  698.0 277.7 %all-reduce.3.cloned.1.call-done = f32[256,24,64]{0,2,1:T(8,128)} async-done(((f32[256,24,64]{0,2,1:T(8,128)}), f32[256,24,64]{0,2,1:T(8,128)}) %all-reduce.3.cloned.1.call-update) | async-done | bytes 1572880 | tf_op jit(solution)/shard_map/psum | solution.py:100
  975.7 1.6 divide_convert_fusion.2
  977.3 15.7 %while.25 = (s32[]{:T(128)}, f32[3,128,8,64]{1,3,2,0:T(8,128)}, s32[3]{0:T(128)S(1)}, bf16[256,24,64]{0,2,1:T(8,128)(2,1)S(1)}, bf16[128,24,64]{0,2,1:T(8,128)(2...) while((s32[]{:T(128)}, f32[3,128,8,64]{1,3,2,0:T(8,128)}, ...), condition=%wide.region_12.13_spmd, body=%wide.region_9.12_spmd.sunk | while | flops 102499840 | bytes 1322151 | solution.py:115
  977.3 0.6 dynamic_slice.80
  978.6 1.6 fusion.76
  980.2 2.4 fusion.77
  982.6 0.6 dynamic_slice.80
  983.8 1.6 fusion.76
  985.4 2.4 fusion.77
  987.8 0.6 dynamic_slice.80
  989.1 1.6 fusion.76
  990.6 2.4 fusion.77
  993.1 1.7 copy.30
  995.0 1.3 reshape.100
  996.5 5.4 fusion.46
  (80 shorter events, 2.4 us)
Async XLA Ops:
  6.5 15.1 %copy-start.4 = (bf16[1,4,1,32,1536]{4,3,2,1,0:T(8,128)(2,1)S(1)}, bf16[1,4,1,32,1536]{4,3,2,1,0:T(8,128)(2,1)}, u32[]{:S(2)}) copy-start(bf16[1,4,1,32,1536]{4,3,2,1,0:T(8,128)(2,1)} %param.9) | copy-start | bytes 1179652
  8.8 35.8 %all-to-all-start = ((bf16[64,4,1536]{2,1,0:T(4,128)(2,1)}), bf16[64,4,1536]{2,1,0:T(4,128)(2,1)S(1)}, u32[]{:S(2)}, u32[]{:S(2)}) async-start(bf16[64,4,1536]{2,1,0:T(4,128)(2,1)} %stack.2), calls=%async_computation | async-start | bytes 1572864 | tf_op jit(solution)/shard_map/all_to_all | solution.py:19
  21.6 1.1 copy-start
  21.6 954.2 %all-reduce.3.cloned.1.call-start = ((), (), s32[]{:S(2)}) async-start(), calls=%async_computation.1 | async-start | bytes 3145728 | tf_op jit(solution)/shard_map/psum | solution.py:100
  366.0 16.4 %copy-start.1 = (bf16[1,4,1,32,1536]{4,3,2,1,0:T(8,128)(2,1)S(1)}, bf16[1,4,1,32,1536]{4,3,2,1,0:T(8,128)(2,1)}, u32[]{:S(2)}) copy-start(bf16[1,4,1,32,1536]{4,3,2,1,0:T(8,128)(2,1)} %param.8) | copy-start | bytes 1179652
  366.1 7.9 collective-permute-start.1
  368.1 7.5 collective-permute-start
  374.0 1.7 copy-start.2
  375.6 1.4 copy-start.3
  375.7 14.1 %collective-permute-start.3 = (bf16[1,6,1,32,1536]{4,3,1,2,0:T(8,128)(2,1)S(1)}, bf16[1,6,1,32,1536]{4,3,1,2,0:T(8,128)(2,1)S(1)}, u32[]{:S(2)}, u32[]{:S(2)}) collective-permute-start(bf16[1,6,1,32,1536]{4,3,1,2,0:T(8,128)(2,1)S(1)} %pad_maximum_fusion), channel_id=1, source_target_pairs={{1,0},{2,1},{3,2},{4,3},{5,4},{6,5},{7,6},{8,7},{9,8},{10,9},{11,1... | collective-permute-start | bytes 1769480 | tf_op jit(solution)/shard_map/ppermute | solution.py:33
  377.0 13.9 %collective-permute-start.2 = (bf16[1,6,1,32,1536]{4,3,1,2,0:T(8,128)(2,1)S(1)}, bf16[1,6,1,32,1536]{4,3,1,2,0:T(8,128)(2,1)}, u32[]{:S(2)}, u32[]{:S(2)}) collective-permute-start(bf16[1,6,1,32,1536]{4,3,1,2,0:T(8,128)(2,1)S(1)} %pad_maximum_fusion), channel_id=1, source_target_pairs={{0,1},{1,2},{2,3},{3,4},{4,5},{5,6},{6,7},{7,8},{8,9},{9,10},{10,1... | collective-permute-start | bytes 1769480 | tf_op jit(solution)/shard_map/ppermute | solution.py:31
  994.7 1.5 copy-start.5
  994.8 1.5 copy-start.6
  994.8 1.5 copy-start.7
  994.8 1.5 copy-start.8
  994.8 1.5 copy-start.9
  994.8 1.5 copy-start.10
  994.8 1.5 copy-start.11
  994.8 1.5 copy-start.12
  994.8 1.5 copy-start.13
  994.8 1.5 copy-start.14
  994.8 1.5 copy-start.15
  994.9 1.5 copy-start.16
  994.9 1.5 copy-start.17
  994.9 1.5 copy-start.18
  994.9 1.5 copy-start.19
  994.9 1.5 copy-start.20
  994.9 1.5 copy-start.21
  994.9 1.5 copy-start.22
  994.9 1.5 copy-start.23
  994.9 1.5 copy-start.24
  994.9 1.5 copy-start.25
  995.0 1.5 copy-start.26
  995.0 1.5 copy-start.27
  995.0 1.5 copy-start.28
Sparse Core Ops, SparseCore 0:
  366.1 609.5 all-reduce.2
